TPU v7x, 32 devices: a whole 2x2x4 slice. The times are simulated.
32 devices in a mesh: dp: 8 (over z, x), sp: 4 (over y, core).
Axes of the slice: x: 2, y: 2, z: 4, core: 2. Of those that a mesh axis runs over, the one named last changes fastest.
Arguments:
- tokens: bfloat16 [16, 1024, 768], P('dp', 'sp'), may hold values from -6 to 6
- segment_ids: int32 [16, 1024], P('dp'), may hold values from 0 to 15, never falling along the last dimension, each value on 1 to 512 neighbouring positions
- key_mask: int32 [16, 1024], P('dp'), may hold values 0 or 1
- w_query: bfloat16 [768, 768], P('dp'), may hold values from -0.3125 to 0.3125
- b_query: bfloat16 [768], P('dp'), may hold values from -3 to 3
- w_key: bfloat16 [768, 768], P('dp'), may hold values from -0.3125 to 0.3125
- w_value: bfloat16 [768, 768], P('dp'), may hold values from -0.21875 to 0.21875
- b_value: bfloat16 [768], P('dp'), may hold values from -2 to 2
- w_attn_out: bfloat16 [768, 768], P('dp'), may hold values from -0.625 to 0.625
- b_attn_out: bfloat16 [768], P('dp'), may hold values from -2 to 2
- gain_attn: bfloat16 [768], P('dp'), may hold values from 0.5 to 1.5
- shift_attn: bfloat16 [768], P('dp'), may hold values from -2 to 2
- w_inner: bfloat16 [768, 3072], P('dp'), may hold values from -0.21875 to 0.21875
- b_inner: bfloat16 [3072], P('dp'), may hold values from -3 to 3
- w_outer: bfloat16 [3072, 768], P('dp'), may hold values from -0.15625 to 0.15625
- b_outer: bfloat16 [768], P('dp'), may hold values from -2 to 2
- gain_ffn: bfloat16 [768], P('dp'), may hold values from 0.5 to 1.5
- shift_ffn: bfloat16 [768], P('dp'), may hold values from -2 to 2
- grad_output: bfloat16 [16, 1024, 768], P('dp', 'sp'), may hold values from -6 to 6
Outputs:
- layer_out: bfloat16 [16, 1024, 768], P('dp', 'sp')
- grad_tokens: bfloat16 [16, 1024, 768], P('dp', 'sp')
- grad_w_query: float32 [768, 768], P('dp')
- grad_b_query: float32 [768], P('dp')
- grad_w_key: float32 [768, 768], P('dp')
- grad_w_value: float32 [768, 768], P('dp')
- grad_b_value: float32 [768], P('dp')
- grad_w_attn_out: float32 [768, 768], P('dp')
- grad_b_attn_out: float32 [768], P('dp')
- grad_gain_attn: float32 [768], P('dp')
- grad_shift_attn: float32 [768], P('dp')
- grad_w_inner: float32 [768, 3072], P('dp')
- grad_b_inner: float32 [3072], P('dp')
- grad_w_outer: float32 [3072, 768], P('dp')
- grad_b_outer: float32 [768], P('dp')
- grad_gain_ffn: float32 [768], P('dp')
- grad_shift_ffn: float32 [768], P('dp')
Inputs may be any that keep to these rules, and one draw needn't show every extreme that they name: `segment_ids`: along each sequence the ids never fall; each id marks one document of 1 to 512 tokens, and in every sequence one document has exactly 512. `key_mask`: 0 marks a padding token, which only it itself attends to.
All inputs are finite; a program needn't handle non-finite values. No bound on the sum of `key_mask` on one device may be relied on, other than what follows from the above.
Results may differ from a plain program's by a relative error of at most 0.018.
Values may be sent and summed in bfloat16 or wider, within the bound.
A program may use at most 192 MiB of HBM per device.

v0:
```python
import jax
import jax.numpy as jnp
from jax import lax
from jax.sharding import PartitionSpec as P

H = 12
HD = 64


EPSILON = 1e-06
MASKED_SCORE = -1e30


def normalize(summed, gain_vec, shift_vec):
    center = jnp.mean(summed, axis=-1, keepdims=True)
    centered = summed - center
    spread = jnp.mean(centered * centered, axis=-1, keepdims=True)
    return centered * lax.rsqrt(spread + EPSILON) * gain_vec + shift_vec


def gelu_exact(inputs_f):
    return jax.nn.gelu(inputs_f, approximate=False)


def matmul(left, right):
    return jnp.dot(left, right, preferred_element_type=jnp.float32)


def left_trans(left, right):
    return lax.dot_general(
        left, right, (((0,), (0,)), ((), ())), preferred_element_type=jnp.float32
    )


def right_trans(left, right):
    return lax.dot_general(
        left, right, (((1,), (1,)), ((), ())), preferred_element_type=jnp.float32
    )


def column_sum(values_low):
    return jnp.sum(values_low, axis=0, dtype=jnp.float32)


def score_block(query_blk, key_heads, seg_query, segments, keepers, pos_query, score_scale):
    scores = (
        jnp.einsum("qhd,khd->hqk", query_blk, key_heads, preferred_element_type=jnp.float32)
        * score_scale
    )
    positions = jnp.arange(segments.shape[0])
    allowed = (seg_query[:, None] == segments[None, :]) & (keepers[None, :] == 1) | (
        pos_query[:, None] == positions[None, :]
    )
    return jnp.where(allowed[None], scores, MASKED_SCORE)


def attend_forward(queries, keys_in, values_in, segments, keepers, head_count, score_scale):
    length = queries.shape[0]
    block_len = min(512, length)
    blocks = length // block_len
    query_heads = queries.reshape(blocks, block_len, head_count, -1)
    key_heads = keys_in.reshape(length, head_count, -1)
    value_heads = values_in.reshape(length, head_count, -1)
    seg_blocks = segments.reshape(blocks, block_len)
    pos_blocks = jnp.arange(length).reshape(blocks, block_len)

    def one_block(member):
        query_blk, seg_query, pos_query = member
        scores = score_block(
            query_blk, key_heads, seg_query, segments, keepers, pos_query, score_scale
        )
        top_score = jnp.max(scores, axis=-1, keepdims=True)
        exponent = jnp.exp(scores - top_score)
        total = jnp.sum(exponent, axis=-1, keepdims=True)
        probability = (exponent / total).astype(jnp.bfloat16)
        attended = jnp.einsum(
            "hqk,khd->qhd", probability, value_heads, preferred_element_type=jnp.float32
        )
        log_total = (top_score + jnp.log(total))[:, :, 0]
        return (attended.reshape(block_len, -1).astype(jnp.bfloat16), log_total)

    attended, log_total = lax.map(one_block, (query_heads, seg_blocks, pos_blocks))
    return (attended.reshape(length, -1), log_total)


def attend_backward(
    queries, keys_in, values_in, grad_att, log_total, segments, keepers, head_count, score_scale
):
    length = queries.shape[0]
    block_len = min(512, length)
    blocks = length // block_len
    query_heads = queries.reshape(blocks, block_len, head_count, -1)
    grad_heads = grad_att.reshape(blocks, block_len, head_count, -1)
    key_heads = keys_in.reshape(length, head_count, -1)
    value_heads = values_in.reshape(length, head_count, -1)
    seg_blocks = segments.reshape(blocks, block_len)
    pos_blocks = jnp.arange(length).reshape(blocks, block_len)

    def one_block(carry, member):
        grad_keys, grad_values = carry
        query_blk, grad_blk, total_blk, seg_query, pos_query = member
        scores = score_block(
            query_blk, key_heads, seg_query, segments, keepers, pos_query, score_scale
        )
        probability = jnp.exp(scores - total_blk[:, :, None])
        grad_prob = jnp.einsum(
            "qhd,khd->hqk", grad_blk, value_heads, preferred_element_type=jnp.float32
        )
        inner_sum = jnp.sum(probability * grad_prob, axis=-1, keepdims=True)
        grad_score = (probability * (grad_prob - inner_sum)).astype(jnp.bfloat16)
        grad_query = (
            jnp.einsum("hqk,khd->qhd", grad_score, key_heads, preferred_element_type=jnp.float32)
            * score_scale
        )
        grad_keys = (
            grad_keys
            + jnp.einsum("hqk,qhd->khd", grad_score, query_blk, preferred_element_type=jnp.float32)
            * score_scale
        )
        grad_values = grad_values + jnp.einsum(
            "hqk,qhd->khd",
            probability.astype(jnp.bfloat16),
            grad_blk,
            preferred_element_type=jnp.float32,
        )
        return ((grad_keys, grad_values), grad_query.reshape(block_len, -1).astype(jnp.bfloat16))

    zeroed = jnp.zeros(key_heads.shape, jnp.float32)
    (grad_keys, grad_values), grad_query = lax.scan(
        one_block, (zeroed, zeroed), (query_heads, grad_heads, log_total, seg_blocks, pos_blocks)
    )
    return (
        grad_query.reshape(length, -1),
        grad_keys.reshape(length, -1).astype(jnp.bfloat16),
        grad_values.reshape(length, -1).astype(jnp.bfloat16),
    )


def layer_pass(tokens, segment_ids, key_mask, shard_params, grad_output):
    (
        w_query,
        b_query,
        w_key,
        w_value,
        b_value,
        w_attn_out,
        b_attn_out,
        gain_attn,
        shift_attn,
        w_inner,
        b_inner,
        w_outer,
        b_outer,
        gain_ffn,
        shift_ffn,
    ) = shard_params
    seq_count, local_len, model_width = tokens.shape
    head_count = H // lax.axis_size("sp")
    score_scale = HD ** (-0.5)
    attn_full = (
        lax.all_gather(w_query, "dp", axis=0, tiled=True),
        lax.all_gather(b_query, "dp", axis=0, tiled=True),
        lax.all_gather(w_key, "dp", axis=0, tiled=True),
        lax.all_gather(w_value, "dp", axis=0, tiled=True),
        lax.all_gather(b_value, "dp", axis=0, tiled=True),
        lax.all_gather(w_attn_out, "dp", axis=0, tiled=True),
        lax.all_gather(b_attn_out, "dp", axis=0, tiled=True),
        lax.all_gather(gain_attn, "dp", axis=0, tiled=True),
        lax.all_gather(shift_attn, "dp", axis=0, tiled=True),
    )
    ffn_full = (
        lax.all_gather(w_inner, "dp", axis=0, tiled=True),
        lax.all_gather(b_inner, "dp", axis=0, tiled=True),
        lax.all_gather(w_outer, "dp", axis=0, tiled=True),
        lax.all_gather(b_outer, "dp", axis=0, tiled=True),
        lax.all_gather(gain_ffn, "dp", axis=0, tiled=True),
        lax.all_gather(shift_ffn, "dp", axis=0, tiled=True),
    )
    (
        full_query,
        full_bquery,
        full_key,
        full_value,
        full_bvalue,
        full_out,
        full_bout,
        full_gain1,
        full_shift1,
    ) = attn_full
    full_inner, full_binner, full_outer, full_bouter, full_gain2, full_shift2 = ffn_full
    token_rows = tokens.reshape(-1, model_width)
    local_shape = (seq_count, local_len, model_width)
    query_low = (
        (matmul(token_rows, full_query) + full_bquery).astype(jnp.bfloat16).reshape(local_shape)
    )
    keys_low = matmul(token_rows, full_key).astype(jnp.bfloat16).reshape(local_shape)
    values_low = (
        (matmul(token_rows, full_value) + full_bvalue).astype(jnp.bfloat16).reshape(local_shape)
    )
    head_query, head_keys, head_values = (
        lax.all_to_all(query_low, "sp", split_axis=2, concat_axis=1, tiled=True),
        lax.all_to_all(keys_low, "sp", split_axis=2, concat_axis=1, tiled=True),
        lax.all_to_all(values_low, "sp", split_axis=2, concat_axis=1, tiled=True),
    )

    def forward_sequence(member):
        return attend_forward(*member, head_count, score_scale)

    attended, log_total = lax.map(
        forward_sequence, (head_query, head_keys, head_values, segment_ids, key_mask)
    )
    merged = lax.all_to_all(attended, "sp", split_axis=1, concat_axis=2, tiled=True)
    merged_rows = merged.reshape(-1, model_width)
    branch = matmul(merged_rows, full_out) + full_bout
    first_sum = token_rows + branch
    hidden, attn_norm_pull = jax.vjp(
        normalize, first_sum, full_gain1.astype(jnp.float32), full_shift1.astype(jnp.float32)
    )
    hidden_low = hidden.astype(jnp.bfloat16)
    inner = matmul(hidden_low, full_inner) + full_binner
    active, gelu_pull = jax.vjp(gelu_exact, inner)
    active_low = active.astype(jnp.bfloat16)
    outer = matmul(active_low, full_outer) + full_bouter
    second_sum = hidden + outer
    result, ffn_norm_pull = jax.vjp(
        normalize, second_sum, full_gain2.astype(jnp.float32), full_shift2.astype(jnp.float32)
    )
    layer_out = result.astype(jnp.bfloat16).reshape(local_shape)
    back_inner, back_outer = (
        lax.all_gather(w_inner, "dp", axis=0, tiled=True),
        lax.all_gather(w_outer, "dp", axis=0, tiled=True),
    )
    back_query, back_key, back_value, back_out = (
        lax.all_gather(w_query, "dp", axis=0, tiled=True),
        lax.all_gather(w_key, "dp", axis=0, tiled=True),
        lax.all_gather(w_value, "dp", axis=0, tiled=True),
        lax.all_gather(w_attn_out, "dp", axis=0, tiled=True),
    )
    cotangent = grad_output.reshape(-1, model_width).astype(jnp.float32)
    grad_second, grad_gain2, grad_shift2 = ffn_norm_pull(cotangent)
    grad_outer_low = grad_second.astype(jnp.bfloat16)
    grad_bouter = column_sum(grad_outer_low)
    grad_wouter = left_trans(active_low, grad_outer_low)
    grad_active = right_trans(grad_outer_low, back_outer)
    (grad_inner,) = gelu_pull(grad_active)
    grad_inner_low = grad_inner.astype(jnp.bfloat16)
    grad_binner = column_sum(grad_inner_low)
    grad_winner = left_trans(hidden_low, grad_inner_low)
    grad_hidden = grad_second + right_trans(grad_inner_low, back_inner)
    grad_first, grad_gain1, grad_shift1 = attn_norm_pull(grad_hidden)
    grad_branch_low = grad_first.astype(jnp.bfloat16)
    grad_bout = column_sum(grad_branch_low)
    grad_wout = left_trans(merged_rows, grad_branch_low)
    grad_merged = right_trans(grad_branch_low, back_out).astype(jnp.bfloat16).reshape(local_shape)
    grad_heads = lax.all_to_all(grad_merged, "sp", split_axis=2, concat_axis=1, tiled=True)

    def backward_sequence(member):
        return attend_backward(*member, head_count, score_scale)

    head_gquery, head_gkeys, head_gvalues = lax.map(
        backward_sequence,
        (head_query, head_keys, head_values, grad_heads, log_total, segment_ids, key_mask),
    )
    grad_query, grad_keys, grad_values = (
        lax.all_to_all(head_gquery, "sp", split_axis=1, concat_axis=2, tiled=True),
        lax.all_to_all(head_gkeys, "sp", split_axis=1, concat_axis=2, tiled=True),
        lax.all_to_all(head_gvalues, "sp", split_axis=1, concat_axis=2, tiled=True),
    )
    grad_query = grad_query.reshape(-1, model_width)
    grad_keys = grad_keys.reshape(-1, model_width)
    grad_values = grad_values.reshape(-1, model_width)
    grad_wquery = left_trans(token_rows, grad_query)
    grad_bquery = column_sum(grad_query)
    grad_wkey = left_trans(token_rows, grad_keys)
    grad_wvalue = left_trans(token_rows, grad_values)
    grad_bvalue = column_sum(grad_values)
    grad_input = (
        grad_first
        + right_trans(grad_query, back_query)
        + right_trans(grad_keys, back_key)
        + right_trans(grad_values, back_value)
    )
    grad_tokens = grad_input.astype(jnp.bfloat16).reshape(local_shape)
    grads = (
        grad_wquery,
        grad_bquery,
        grad_wkey,
        grad_wvalue,
        grad_bvalue,
        grad_wout,
        grad_bout,
        grad_gain1,
        grad_shift1,
        grad_winner,
        grad_binner,
        grad_wouter,
        grad_bouter,
        grad_gain2,
        grad_shift2,
    )
    return (layer_out, grad_tokens, grads)


def body(
    tokens,
    segment_ids,
    key_mask,
    w_query,
    b_query,
    w_key,
    w_value,
    b_value,
    w_attn_out,
    b_attn_out,
    gain_attn,
    shift_attn,
    w_inner,
    b_inner,
    w_outer,
    b_outer,
    gain_ffn,
    shift_ffn,
    grad_output,
):
    shard_params = (
        w_query,
        b_query,
        w_key,
        w_value,
        b_value,
        w_attn_out,
        b_attn_out,
        gain_attn,
        shift_attn,
        w_inner,
        b_inner,
        w_outer,
        b_outer,
        gain_ffn,
        shift_ffn,
    )
    dp_count = lax.axis_size("dp")
    zeroed = tuple(
        (
            jnp.zeros((member.shape[0] * dp_count,) + member.shape[1:], jnp.float32)
            for member in shard_params
        )
    )

    def one_sequence(totals, member):
        seq_tokens, seq_segments, seq_mask, seq_grad = member
        seq_out, seq_gtok, seq_grads = layer_pass(
            seq_tokens[None], seq_segments[None], seq_mask[None], shard_params, seq_grad[None]
        )
        totals = tuple((first + second for first, second in zip(totals, seq_grads)))
        return (totals, (seq_out[0], seq_gtok[0]))

    grads, (layer_out, grad_tokens) = lax.scan(
        one_sequence, zeroed, (tokens, segment_ids, key_mask, grad_output)
    )
    g_wq, g_bq, g_wk, g_wv, g_bv, g_wo, g_bo, g_ga, g_sa, g_wi, g_bi, g_wu, g_bu, g_gf, g_sf = grads
    shards = (
        lax.psum_scatter(g_wq, "dp", scatter_dimension=0, tiled=True),
        lax.psum_scatter(g_bq, "dp", scatter_dimension=0, tiled=True),
        lax.psum_scatter(g_wk, "dp", scatter_dimension=0, tiled=True),
        lax.psum_scatter(g_wv, "dp", scatter_dimension=0, tiled=True),
        lax.psum_scatter(g_bv, "dp", scatter_dimension=0, tiled=True),
        lax.psum_scatter(g_wo, "dp", scatter_dimension=0, tiled=True),
        lax.psum_scatter(g_bo, "dp", scatter_dimension=0, tiled=True),
        lax.psum_scatter(g_ga, "dp", scatter_dimension=0, tiled=True),
        lax.psum_scatter(g_sa, "dp", scatter_dimension=0, tiled=True),
        lax.psum_scatter(g_wi, "dp", scatter_dimension=0, tiled=True),
        lax.psum_scatter(g_bi, "dp", scatter_dimension=0, tiled=True),
        lax.psum_scatter(g_wu, "dp", scatter_dimension=0, tiled=True),
        lax.psum_scatter(g_bu, "dp", scatter_dimension=0, tiled=True),
        lax.psum_scatter(g_gf, "dp", scatter_dimension=0, tiled=True),
        lax.psum_scatter(g_sf, "dp", scatter_dimension=0, tiled=True),
    )
    s_wq, s_bq, s_wk, s_wv, s_bv, s_wo, s_bo, s_ga, s_sa, s_wi, s_bi, s_wu, s_bu, s_gf, s_sf = (
        shards
    )
    summed = (
        lax.psum(s_wq.astype(jnp.bfloat16), "sp").astype(jnp.float32),
        lax.psum(s_bq.astype(jnp.bfloat16), "sp").astype(jnp.float32),
        lax.psum(s_wk.astype(jnp.bfloat16), "sp").astype(jnp.float32),
        lax.psum(s_wv.astype(jnp.bfloat16), "sp").astype(jnp.float32),
        lax.psum(s_bv.astype(jnp.bfloat16), "sp").astype(jnp.float32),
        lax.psum(s_wo.astype(jnp.bfloat16), "sp").astype(jnp.float32),
        lax.psum(s_bo.astype(jnp.bfloat16), "sp").astype(jnp.float32),
        lax.psum(s_ga.astype(jnp.bfloat16), "sp").astype(jnp.float32),
        lax.psum(s_sa.astype(jnp.bfloat16), "sp").astype(jnp.float32),
        lax.psum(s_wi.astype(jnp.bfloat16), "sp").astype(jnp.float32),
        lax.psum(s_bi.astype(jnp.bfloat16), "sp").astype(jnp.float32),
        lax.psum(s_wu.astype(jnp.bfloat16), "sp").astype(jnp.float32),
        lax.psum(s_bu.astype(jnp.bfloat16), "sp").astype(jnp.float32),
        lax.psum(s_gf.astype(jnp.bfloat16), "sp").astype(jnp.float32),
        lax.psum(s_sf.astype(jnp.bfloat16), "sp").astype(jnp.float32),
    )
    (
        out_wq,
        out_bq,
        out_wk,
        out_wv,
        out_bv,
        out_wo,
        out_bo,
        out_ga,
        out_sa,
        out_wi,
        out_bi,
        out_wu,
        out_bu,
        out_gf,
        out_sf,
    ) = summed
    return (
        layer_out,
        grad_tokens,
        out_wq,
        out_bq,
        out_wk,
        out_wv,
        out_bv,
        out_wo,
        out_bo,
        out_ga,
        out_sa,
        out_wi,
        out_bi,
        out_wu,
        out_bu,
        out_gf,
        out_sf,
    )


def solution(mesh):
    return jax.shard_map(
        body,
        mesh=mesh,
        in_specs=(
            P("dp", "sp", None),
            P("dp", None),
            P("dp", None),
            P("dp", None),
            P("dp"),
            P("dp", None),
            P("dp", None),
            P("dp"),
            P("dp", None),
            P("dp"),
            P("dp"),
            P("dp"),
            P("dp", None),
            P("dp"),
            P("dp", None),
            P("dp"),
            P("dp"),
            P("dp"),
            P("dp", "sp", None),
        ),
        out_specs=(
            P("dp", "sp", None),
            P("dp", "sp", None),
            P("dp", None),
            P("dp"),
            P("dp", None),
            P("dp", None),
            P("dp"),
            P("dp", None),
            P("dp"),
            P("dp"),
            P("dp"),
            P("dp", None),
            P("dp"),
            P("dp", None),
            P("dp"),
            P("dp"),
            P("dp"),
        ),
        check_vma=False,
    )
```

profile of v0, /device:TPU:0, one launch (start us, length us, event | category | flops | bytes accessed | tf_op | source)
XLA Modules:
  0.0 1624.6 jit_solution(10727773919756238030)
XLA Ops:
  8.2 928.9 %while.94 = (s32[]{:T(128)}, f32[768,768]{1,0:T(8,128)}, f32[768]{0:T(1024)}, f32[768,768]{1,0:T(8,128)}, f32[768,768]{1,0:T(8,128)}, /*index=5*/f32[768]{0:T(10...) while((s32[]{:T(128)}, f32[768,768]{1,0:T(8,128)}, ...), condition=%wide.region_25.26_spmd.clone, body=%wide.region_0.25_spmd.clone.sunk | while | flops 12425620480 | bytes 488251520 | solution.py:358
  20.7 39.9 %all-reduce.30 = (bf16[768]{0:T(1024)(128)(2,1)S(1)}, bf16[768]{0:T(1024)(128)(2,1)S(1)}, bf16[768]{0:T(1024)(128)(2,1)}, bf16[768]{0:T(1024)(128)(2,1)}, bf16[7...) all-reduce(bf16[768]{0:T(1024)(128)(2,1)S(1)} %dynamic-update-slice, ...), channel_id=1, replica_groups=mesh['dp'=8,'sp'=4] {'dp'}, use_global_device_ids=true, to_apply=%add | all-reduce | flops 6144 | bytes 24576 | tf_op jit(solution)/shard_map/while
  70.9 26.8 %all-gather.15.cloned.1.call-done = bf16[768,768]{1,0:T(8,128)(2,1)} async-done(((bf16[96,768]{1,0:T(8,128)(2,1)}), bf16[768,768]{1,0:T(8,128)(2,1)}) %all-gather.15.cloned.1.call-update) | async-done | bytes 1179664 | tf_op jit(solution)/shard_map/while/body/eval_jaxpr/all_gather | solution.py:164
  108.5 31.1 %all-gather.13.cloned.1.call-done = bf16[768,768]{1,0:T(8,128)(2,1)} async-done(((bf16[96,768]{1,0:T(8,128)(2,1)}), bf16[768,768]{1,0:T(8,128)(2,1)}) %all-gather.13.cloned.1.call-update) | async-done | bytes 1179664 | tf_op jit(solution)/shard_map/while/body/eval_jaxpr/all_gather | solution.py:163
  158.8 12.4 while.95
  189.3 26.7 %all-gather.3 = bf16[8,1,384]{2,1,0:T(2,128)(2,1)S(1)} all-gather(bf16[1,1,384]{2,1,0:T(2,128)(2,1)S(1)} %reshape.555), channel_id=1, replica_groups=mesh['dp'=8,'sp'=4] {'dp'}, dimensions={0}, use_global_device_ids=true | all-gather | bytes 6912 | tf_op jit(solution)/shard_map/while/body/eval_jaxpr/all_gather | solution.py:173
  226.0 35.8 %all-gather.19.cloned.1.call-done = bf16[768,3072]{1,0:T(8,128)(2,1)} async-done(((bf16[96,3072]{1,0:T(8,128)(2,1)}), bf16[768,3072]{1,0:T(8,128)(2,1)}) %all-gather.19.cloned.1.call-update) | async-done | bytes 4718608 | tf_op jit(solution)/shard_map/while/body/eval_jaxpr/all_gather | solution.py:172
  261.9 11.7 multiply_convert_fusion.4
  273.5 68.1 %all-gather.21.cloned.1.call-done = bf16[3072,768]{1,0:T(8,128)(2,1)} async-done(((bf16[384,768]{1,0:T(8,128)(2,1)}), bf16[3072,768]{1,0:T(8,128)(2,1)}) %all-gather.21.cloned.1.call-update) | async-done | bytes 4718608 | tf_op jit(solution)/shard_map/while/body/eval_jaxpr/all_gather | solution.py:174
  371.8 6.8 select_add_fusion.34
  378.7 5.2 select_add_fusion.36
  387.3 21.6 %while.96 = (s32[]{:T(128)}, f32[1024,3,64]{0,2,1:T(8,128)S(1)}, f32[1024,3,64]{0,2,1:T(8,128)}, bf16[2,512,192]{1,2,0:T(8,128)(2,1)S(1)}, bf16[2,512,3,64]{1,3,...) while((s32[]{:T(128)}, f32[1024,3,64]{0,2,1:T(8,128)S(1)}, ...), condition=%wide.region_15.15_spmd.clone, body=%wide.region_13.14_spmd.clone.sunk | while | flops 1033502208 | bytes 61346032 | solution.py:129
  413.5 4.9 reduce.31
  481.6 35.4 %all-reduce.30 = (bf16[768]{0:T(1024)(128)(2,1)S(1)}, bf16[768]{0:T(1024)(128)(2,1)S(1)}, bf16[768]{0:T(1024)(128)(2,1)}, bf16[768]{0:T(1024)(128)(2,1)}, bf16[7...) all-reduce(bf16[768]{0:T(1024)(128)(2,1)S(1)} %dynamic-update-slice, ...), channel_id=1, replica_groups=mesh['dp'=8,'sp'=4] {'dp'}, use_global_device_ids=true, to_apply=%add | all-reduce | flops 6144 | bytes 24576 | tf_op jit(solution)/shard_map/while
  527.3 25.9 %all-gather.15.cloned.1.call-done = bf16[768,768]{1,0:T(8,128)(2,1)} async-done(((bf16[96,768]{1,0:T(8,128)(2,1)}), bf16[768,768]{1,0:T(8,128)(2,1)}) %all-gather.15.cloned.1.call-update) | async-done | bytes 1179664 | tf_op jit(solution)/shard_map/while/body/eval_jaxpr/all_gather | solution.py:164
  564.0 31.1 %all-gather.13.cloned.1.call-done = bf16[768,768]{1,0:T(8,128)(2,1)} async-done(((bf16[96,768]{1,0:T(8,128)(2,1)}), bf16[768,768]{1,0:T(8,128)(2,1)}) %all-gather.13.cloned.1.call-update) | async-done | bytes 1179664 | tf_op jit(solution)/shard_map/while/body/eval_jaxpr/all_gather | solution.py:163
  614.3 12.4 while.95
  644.8 26.9 %all-gather.3 = bf16[8,1,384]{2,1,0:T(2,128)(2,1)S(1)} all-gather(bf16[1,1,384]{2,1,0:T(2,128)(2,1)S(1)} %reshape.555), channel_id=1, replica_groups=mesh['dp'=8,'sp'=4] {'dp'}, dimensions={0}, use_global_device_ids=true | all-gather | bytes 6912 | tf_op jit(solution)/shard_map/while/body/eval_jaxpr/all_gather | solution.py:173
  682.4 35.5 %all-gather.19.cloned.1.call-done = bf16[768,3072]{1,0:T(8,128)(2,1)} async-done(((bf16[96,3072]{1,0:T(8,128)(2,1)}), bf16[768,3072]{1,0:T(8,128)(2,1)}) %all-gather.19.cloned.1.call-update) | async-done | bytes 4718608 | tf_op jit(solution)/shard_map/while/body/eval_jaxpr/all_gather | solution.py:172
  717.9 11.7 multiply_convert_fusion.4
  729.6 67.7 %all-gather.21.cloned.1.call-done = bf16[3072,768]{1,0:T(8,128)(2,1)} async-done(((bf16[384,768]{1,0:T(8,128)(2,1)}), bf16[3072,768]{1,0:T(8,128)(2,1)}) %all-gather.21.cloned.1.call-update) | async-done | bytes 4718608 | tf_op jit(solution)/shard_map/while/body/eval_jaxpr/all_gather | solution.py:174
  827.5 9.6 select_add_fusion.34
  837.1 8.9 select_add_fusion.36
  849.4 21.6 %while.96 = (s32[]{:T(128)}, f32[1024,3,64]{0,2,1:T(8,128)S(1)}, f32[1024,3,64]{0,2,1:T(8,128)}, bf16[2,512,192]{1,2,0:T(8,128)(2,1)S(1)}, bf16[2,512,3,64]{1,3,...) while((s32[]{:T(128)}, f32[1024,3,64]{0,2,1:T(8,128)S(1)}, ...), condition=%wide.region_15.15_spmd.clone, body=%wide.region_13.14_spmd.clone.sunk | while | flops 1033502208 | bytes 61346032 | solution.py:129
  941.1 67.1 %reduce-scatter.7.cloned.1.call-done = f32[96,768]{1,0:T(8,128)} async-done(((f32[768,768]{1,0:T(8,128)}), f32[96,768]{1,0:T(8,128)}) %reduce-scatter.7.cloned.1.call-update) | async-done | bytes 294928 | tf_op jit(solution)/shard_map/reduce_scatter | solution.py:363
  1009.8 70.6 %reduce-scatter.9.cloned.1.call-done = f32[96,768]{1,0:T(8,128)} async-done(((f32[768,768]{1,0:T(8,128)}), f32[96,768]{1,0:T(8,128)}) %reduce-scatter.9.cloned.1.call-update) | async-done | bytes 294928 | tf_op jit(solution)/shard_map/reduce_scatter | solution.py:365
  1082.1 70.7 %reduce-scatter.11.cloned.1.call-done = f32[96,768]{1,0:T(8,128)} async-done(((f32[768,768]{1,0:T(8,128)}), f32[96,768]{1,0:T(8,128)}) %reduce-scatter.11.cloned.1.call-update) | async-done | bytes 294928 | tf_op jit(solution)/shard_map/reduce_scatter | solution.py:366
  1154.5 71.0 %reduce-scatter.13.cloned.1.call-done = f32[96,768]{1,0:T(8,128)} async-done(((f32[768,768]{1,0:T(8,128)}), f32[96,768]{1,0:T(8,128)}) %reduce-scatter.13.cloned.1.call-update) | async-done | bytes 294928 | tf_op jit(solution)/shard_map/reduce_scatter | solution.py:368
  1227.2 163.2 %reduce-scatter.15.cloned.1.call-done = f32[96,3072]{1,0:T(8,128)} async-done(((f32[768,3072]{1,0:T(8,128)}), f32[96,3072]{1,0:T(8,128)}) %reduce-scatter.15.cloned.1.call-update) | async-done | bytes 1179664 | tf_op jit(solution)/shard_map/reduce_scatter | solution.py:372
  1392.5 162.6 %reduce-scatter.17.cloned.1.call-done = f32[384,768]{1,0:T(8,128)} async-done(((f32[3072,768]{1,0:T(8,128)}), f32[384,768]{1,0:T(8,128)}) %reduce-scatter.17.cloned.1.call-update) | async-done | bytes 1179664 | tf_op jit(solution)/shard_map/reduce_scatter | solution.py:374
  1559.2 35.7 %all-reduce.26 = (bf16[768]{0:T(1024)(128)(2,1)S(1)}, bf16[768]{0:T(1024)(128)(2,1)S(1)}, bf16[768]{0:T(1024)(128)(2,1)S(1)}, bf16[768]{0:T(1024)(128)(2,1)S(1)}...) all-reduce(f32[768]{0:T(1024)S(1)} %copy-done.71, ...), channel_id=3, replica_groups=mesh['dp'=8,'sp'=4] {'dp'}, use_global_device_ids=true, to_apply=%region_28.29.clone | all-reduce | flops 9216 | bytes 55296
  1595.6 6.7 all-reduce.27
  (830 shorter events, 442.2 us)
Async XLA Ops:
  8.6 52.0 %all-gather.11.cloned.1.call-start = ((), (), s32[]{:S(2)}) async-start(), calls=%async_computation.21 | async-start | bytes 1327104 | tf_op jit(solution)/shard_map/while/body/eval_jaxpr/all_gather | solution.py:161
  9.3 88.4 %all-gather.15.cloned.1.call-start = ((), (), s32[]{:S(2)}) async-start(), calls=%async_computation.23 | async-start | bytes 1327104 | tf_op jit(solution)/shard_map/while/body/eval_jaxpr/all_gather | solution.py:164
  10.1 129.6 %all-gather.13.cloned.1.call-start = ((), (), s32[]{:S(2)}) async-start(), calls=%async_computation.22 | async-start | bytes 1327104 | tf_op jit(solution)/shard_map/while/body/eval_jaxpr/all_gather | solution.py:163
  10.8 213.0 %all-gather.17.cloned.1.call-start = ((), (), s32[]{:S(2)}) async-start(), calls=%async_computation.24 | async-start | bytes 1327104 | tf_op jit(solution)/shard_map/while/body/eval_jaxpr/all_gather | solution.py:166
  11.4 250.5 %all-gather.19.cloned.1.call-start = ((), (), s32[]{:S(2)}) async-start(), calls=%async_computation.25 | async-start | bytes 5308416 | tf_op jit(solution)/shard_map/while/body/eval_jaxpr/all_gather | solution.py:172
  67.4 37.1 %all-to-all-start = ((bf16[4,2,24576]{2,1,0:T(2,128)(2,1)}), bf16[4,2,24576]{2,1,0:T(2,128)(2,1)S(1)}, u32[]{:S(2)}, u32[]{:S(2)}) async-start(bf16[4,2,24576]{2,1,0:T(2,128)(2,1)} %reshape.542), calls=%async_computation | async-start | bytes 786432 | tf_op jit(solution)/shard_map/while/body/eval_jaxpr/all_to_all | solution.py:201
  104.5 42.0 %all-to-all-start.2 = ((bf16[4,2,24576]{2,1,0:T(2,128)(2,1)}), bf16[4,2,24576]{2,1,0:T(2,128)(2,1)S(1)}, u32[]{:S(2)}, u32[]{:S(2)}) async-start(bf16[4,2,24576]{2,1,0:T(2,128)(2,1)} %reshape.549), calls=%async_computation.2 | async-start | bytes 786432 | tf_op jit(solution)/shard_map/while/body/eval_jaxpr/all_to_all | solution.py:203
  108.0 233.7 %all-gather.21.cloned.1.call-start = ((), (), s32[]{:S(2)}) async-start(), calls=%async_computation.26 | async-start | bytes 5308416 | tf_op jit(solution)/shard_map/while/body/eval_jaxpr/all_gather | solution.py:174
  178.2 40.1 %all-to-all-start.3 = ((bf16[4,2,24576]{2,1,0:T(2,128)(2,1)}), bf16[4,2,24576]{2,1,0:T(2,128)(2,1)S(1)}, u32[]{:S(2)}, u32[]{:S(2)}) async-start(bf16[4,2,24576]{2,1,0:T(2,128)(2,1)} %reshape.553), calls=%async_computation.3 | async-start | bytes 786432 | tf_op jit(solution)/shard_map/while/body/eval_jaxpr/all_to_all | solution.py:212
  367.7 16.8 %all-to-all-start.4 = ((bf16[4,2,24576]{2,1,0:T(2,128)(2,1)}), bf16[4,2,24576]{2,1,0:T(2,128)(2,1)}, u32[]{:S(2)}, u32[]{:S(2)}) async-start(bf16[4,2,24576]{2,1,0:T(2,128)(2,1)} %reshape.556), calls=%async_computation.4 | async-start | bytes 786432 | tf_op jit(solution)/shard_map/while/body/eval_jaxpr/all_to_all | solution.py:255
  419.7 14.2 all-to-all-start.5
  433.9 11.5 all-to-all-start.7
  445.5 11.6 all-to-all-start.6
  469.3 47.7 %all-gather.11.cloned.1.call-start = ((), (), s32[]{:S(2)}) async-start(), calls=%async_computation.21 | async-start | bytes 1327104 | tf_op jit(solution)/shard_map/while/body/eval_jaxpr/all_gather | solution.py:161
  470.1 83.1 %all-gather.15.cloned.1.call-start = ((), (), s32[]{:S(2)}) async-start(), calls=%async_computation.23 | async-start | bytes 1327104 | tf_op jit(solution)/shard_map/while/body/eval_jaxpr/all_gather | solution.py:164
  470.8 124.4 %all-gather.13.cloned.1.call-start = ((), (), s32[]{:S(2)}) async-start(), calls=%async_computation.22 | async-start | bytes 1327104 | tf_op jit(solution)/shard_map/while/body/eval_jaxpr/all_gather | solution.py:163
  471.5 208.6 %all-gather.17.cloned.1.call-start = ((), (), s32[]{:S(2)}) async-start(), calls=%async_computation.24 | async-start | bytes 1327104 | tf_op jit(solution)/shard_map/while/body/eval_jaxpr/all_gather | solution.py:166
  472.1 245.7 %all-gather.19.cloned.1.call-start = ((), (), s32[]{:S(2)}) async-start(), calls=%async_computation.25 | async-start | bytes 5308416 | tf_op jit(solution)/shard_map/while/body/eval_jaxpr/all_gather | solution.py:172
  523.8 36.1 %all-to-all-start = ((bf16[4,2,24576]{2,1,0:T(2,128)(2,1)}), bf16[4,2,24576]{2,1,0:T(2,128)(2,1)S(1)}, u32[]{:S(2)}, u32[]{:S(2)}) async-start(bf16[4,2,24576]{2,1,0:T(2,128)(2,1)} %reshape.542), calls=%async_computation | async-start | bytes 786432 | tf_op jit(solution)/shard_map/while/body/eval_jaxpr/all_to_all | solution.py:201
  560.0 42.0 %all-to-all-start.2 = ((bf16[4,2,24576]{2,1,0:T(2,128)(2,1)}), bf16[4,2,24576]{2,1,0:T(2,128)(2,1)S(1)}, u32[]{:S(2)}, u32[]{:S(2)}) async-start(bf16[4,2,24576]{2,1,0:T(2,128)(2,1)} %reshape.549), calls=%async_computation.2 | async-start | bytes 786432 | tf_op jit(solution)/shard_map/while/body/eval_jaxpr/all_to_all | solution.py:203
  563.4 233.8 %all-gather.21.cloned.1.call-start = ((), (), s32[]{:S(2)}) async-start(), calls=%async_computation.26 | async-start | bytes 5308416 | tf_op jit(solution)/shard_map/while/body/eval_jaxpr/all_gather | solution.py:174
  633.6 41.0 %all-to-all-start.3 = ((bf16[4,2,24576]{2,1,0:T(2,128)(2,1)}), bf16[4,2,24576]{2,1,0:T(2,128)(2,1)S(1)}, u32[]{:S(2)}, u32[]{:S(2)}) async-start(bf16[4,2,24576]{2,1,0:T(2,128)(2,1)} %reshape.553), calls=%async_computation.3 | async-start | bytes 786432 | tf_op jit(solution)/shard_map/while/body/eval_jaxpr/all_to_all | solution.py:212
  823.3 23.2 %all-to-all-start.4 = ((bf16[4,2,24576]{2,1,0:T(2,128)(2,1)}), bf16[4,2,24576]{2,1,0:T(2,128)(2,1)}, u32[]{:S(2)}, u32[]{:S(2)}) async-start(bf16[4,2,24576]{2,1,0:T(2,128)(2,1)} %reshape.556), calls=%async_computation.4 | async-start | bytes 786432 | tf_op jit(solution)/shard_map/while/body/eval_jaxpr/all_to_all | solution.py:255
  881.8 16.0 all-to-all-start.5
  909.3 11.6 all-to-all-start.6
  937.1 71.1 %reduce-scatter.7.cloned.1.call-start = ((), (), s32[]{:S(2)}) async-start(), calls=%async_computation.14 | async-start | bytes 2654208 | tf_op jit(solution)/shard_map/reduce_scatter | solution.py:363
  937.6 142.8 %reduce-scatter.9.cloned.1.call-start = ((), (), s32[]{:S(2)}) async-start(), calls=%async_computation.15 | async-start | bytes 2654208 | tf_op jit(solution)/shard_map/reduce_scatter | solution.py:365
  938.2 214.6 %reduce-scatter.11.cloned.1.call-start = ((), (), s32[]{:S(2)}) async-start(), calls=%async_computation.16 | async-start | bytes 2654208 | tf_op jit(solution)/shard_map/reduce_scatter | solution.py:366
  938.8 286.7 %reduce-scatter.13.cloned.1.call-start = ((), (), s32[]{:S(2)}) async-start(), calls=%async_computation.17 | async-start | bytes 2654208 | tf_op jit(solution)/shard_map/reduce_scatter | solution.py:368
  939.5 450.8 %reduce-scatter.15.cloned.1.call-start = ((), (), s32[]{:S(2)}) async-start(), calls=%async_computation.18 | async-start | bytes 10616832 | tf_op jit(solution)/shard_map/reduce_scatter | solution.py:372
  940.3 614.8 %reduce-scatter.17.cloned.1.call-start = ((), (), s32[]{:S(2)}) async-start(), calls=%async_computation.19 | async-start | bytes 10616832 | tf_op jit(solution)/shard_map/reduce_scatter | solution.py:374
  941.0 666.0 %all-reduce.33.cloned.1.call-start = ((), (), s32[]{:S(2)}) async-start(), calls=%async_computation.20 | async-start | bytes 3538944 | tf_op jit(solution)/shard_map/psum | solution.py:383
  (166 other events, 6155.3 us)
Sparse Core Ops, SparseCore 0:
  11.6 44.0 all-gather.10
  57.9 39.8 all-gather.14
  99.9 39.7 all-gather.12
  141.7 39.8 all-gather.16
  183.6 78.2 all-gather.18
  263.9 77.6 all-gather.20
  472.3 38.8 all-gather.10
  513.4 39.7 all-gather.14
  555.4 39.7 all-gather.12
  597.2 39.8 all-gather.16
  639.2 78.5 all-gather.18
  719.9 77.3 all-gather.20
Sparse Core Ops, SparseCore 1:
  941.0 67.1 reduce-scatter.6
  1011.5 68.8 reduce-scatter.8
  1083.8 69.0 reduce-scatter.10
  1156.4 69.1 reduce-scatter.12
  1229.2 161.1 reduce-scatter.14
  1394.0 161.0 reduce-scatter.16
  1558.9 45.4 all-reduce.32
where the time goes:
time: 1630 us; the launch traced here: 1620 us
  waiting for transfers between devices  952 us (58%)
  blocking collectives  171 us (10%)
  matrix products  152 us (9%)
  other arithmetic  138 us (8%)
  local copies, waits for them, and re-layouts  126 us (8%)
  starting transfers between devices  60 us (4%)
  between operations  17.4 us (1%)
    reduce_scatter x1, waiting for transfers between devices, body(): lax.psum_scatter(g_wi, 'dp', scatter_dimension=0, tiled=True)  163 us
    reduce_scatter x1, waiting for transfers between devices, body(): lax.psum_scatter(g_wu, 'dp', scatter_dimension=0, tiled=True)  163 us
    all_gather x2, waiting for transfers between devices, layer_pass(): lax.all_gather(w_outer, 'dp', axis=0, tiled=True)  136 us
    while x400, local copies, waits for them, and re-layouts  78.2 us
    while x2, blocking collectives  75.3 us
    all_gather x2, waiting for transfers between devices, layer_pass(): lax.all_gather(w_inner, 'dp', axis=0, tiled=True)  71.3 us
    reduce_scatter x1, waiting for transfers between devices, body(): lax.psum_scatter(g_wo, 'dp', scatter_dimension=0, tiled=True)  71 us
    reduce_scatter x1, waiting for transfers between devices, body(): lax.psum_scatter(g_wv, 'dp', scatter_dimension=0, tiled=True)  70.7 us
  transfers between devices with their start and end apart: 35, of which 18 were waited for; matrix products, arithmetic and copies ran while one was open for 16% of the time, Pallas kernels for 0%

commit v1 on v0

--- a/solution.py
+++ b/solution.py
@@ -1,7 +1,12 @@
 import jax
 import jax.numpy as jnp
 from jax import lax
+from jax.experimental import pallas as pl
+from jax.experimental.pallas import tpu as pltpu
 from jax.sharding import PartitionSpec as P
+
+MESH = pl.DeviceIdType.MESH
+NG = 3
 
 H = 12
 HD = 64
@@ -434,9 +439,312 @@
     )
 
 
+def coords():
+    d = lax.axis_index("dp"); s = lax.axis_index("sp")
+    return d // 2, d % 2, s // 2, s % 2
+
+class AG:
+    NSEM = 28
+    def __init__(self, src, full, send, recv):
+        self.src, self.full, self.send, self.recv = src, full, send, recv
+        self.z, self.x, self.y, self.c = coords()
+        self.pending = []
+    def dev(self, z, x, y, c): return (z * 2 + x, y * 2 + c)
+    def zp(self, dz): return lax.rem(self.z + dz, 4)
+    def copy(self, src, dst, g, sslot, rslot, dev):
+        cp = pltpu.make_async_remote_copy(src_ref=src, dst_ref=dst, send_sem=self.send.at[g, sslot], recv_sem=self.recv.at[g, rslot], device_id=dev, device_id_type=MESH)
+        cp.start()
+        self.pending.append(cp)
+    def wait_recv(self, g, slot, ref):
+        pltpu.make_async_remote_copy(src_ref=ref, dst_ref=ref, send_sem=self.send.at[g, slot], recv_sem=self.recv.at[g, slot], device_id=self.dev(self.z, self.x, self.y, 1 - self.c), device_id_type=MESH).wait_recv()
+    def start_z(self, g):
+        z, x, y, c = self.z, self.x, self.y, self.c
+        q = y * 2 + c; d = z * 2 + x
+        for dz in (1, 3, 2):
+            zt = lax.rem(z + 4 - dz, 4)
+            self.copy(self.src(g, q), self.full(g, d, q), g, dz - 1, dz - 1, self.dev(zt, x, y, c))
+    def start_x(self, g):
+        z, x, y, c = self.z, self.x, self.y, self.c
+        d = z * 2 + x
+        self.copy(self.src(g, y * 2 + c), self.full(g, d, y * 2 + c), g, 3, 3, self.dev(z, 1 - x, y, c))
+        self.copy(self.src(g, (1 - y) * 2 + c), self.full(g, d, (1 - y) * 2 + c), g, 4, 7, self.dev(z, 1 - x, y, c))
+    def piece(self, g, slot):
+        z, x, y, c = self.z, self.x, self.y, self.c
+        if slot < 3: return (self.zp(slot + 1) * 2 + x, y * 2 + c)
+        if slot < 7: return (self.zp(slot - 3) * 2 + 1 - x, y * 2 + c)
+        if slot == 7: return (z * 2 + 1 - x, (1 - y) * 2 + c)
+        if slot < 11: return (self.zp(slot - 7) * 2 + x, (1 - y) * 2 + c)
+        if slot < 14: return (self.zp(slot - 10) * 2 + 1 - x, (1 - y) * 2 + c)
+        dd, qq = self.piece(g, slot - 14)
+        return dd, qq + 1 - 2 * c
+    def on(self, g, slot):
+        z, x, y, c = self.z, self.x, self.y, self.c
+        dd, qq = self.piece(g, slot)
+        ref = self.full(g, dd, qq)
+        self.wait_recv(g, slot, ref)
+        if slot < 3:
+            dz = slot + 1
+            self.copy(ref, ref, g, 4 + dz, 3 + dz, self.dev(z, 1 - x, y, c))
+            self.copy(ref, ref, g, 7 + dz, 7 + dz, self.dev(z, x, 1 - y, c))
+        elif 4 <= slot < 7 and (slot - 3) != 2:
+            dz = slot - 3
+            self.copy(ref, ref, g, 10 + dz, 10 + dz, self.dev(z, x, 1 - y, c))
+        elif 8 <= slot < 11 and (slot - 7) == 2:
+            dz = slot - 7
+            self.copy(ref, ref, g, 10 + dz, 10 + dz, self.dev(z, 1 - x, y, c))
+        if slot < 14:
+            self.copy(ref, ref, g, 14 + slot, 14 + slot, self.dev(z, x, y, 1 - c))
+    def finish(self):
+        for cp in self.pending: cp.wait_send()
+
+def barrier(peers):
+    b = pltpu.get_barrier_semaphore()
+    for p in peers: pl.semaphore_signal(b, inc=1, device_id=p, device_id_type=MESH)
+    pl.semaphore_wait(b, len(peers))
+
+def ag_kernel(wq, wk, wv, wo, wi, wu, f0, f1, f2, send, recv, lsem):
+    def full(g, d, q):
+        if g == 0: return f0.at[q, pl.ds(pl.multiple_of(d * 96, 96), 96), :]
+        if g == 1: return f1.at[q, pl.ds(pl.multiple_of(d * 96, 96), 96), :]
+        return f2.at[pl.ds(pl.multiple_of(d * 384 + q * 96, 96), 96), :]
+    z, x, y, c = coords()
+    d = z * 2 + x
+    loc = []
+    for q, w in enumerate((wq, wk, wv, wo)):
+        loc.append(pltpu.make_async_copy(w, full(0, d, q), lsem.at[q]))
+        loc.append(pltpu.make_async_copy(wi.at[:, pl.ds(q * 768, 768)], full(1, d, q), lsem.at[4 + q]))
+        loc.append(pltpu.make_async_copy(wu.at[pl.ds(q * 96, 96), :], full(2, d, q), lsem.at[8 + q]))
+    def src(g, q):
+        return full(g, d, q)
+    ag = AG(src, full, send, recv)
+    barrier([ag.dev(ag.zp(1), x, y, c), ag.dev(ag.zp(2), x, y, c), ag.dev(ag.zp(3), x, y, c), ag.dev(z, 1 - x, y, c), ag.dev(z, x, 1 - y, c), ag.dev(z, x, y, 1 - c)])
+    for l in loc: l.start()
+    for l in loc: l.wait()
+    ag.start_z(0); ag.start_x(0)
+    for g in range(NG):
+        for slot in (0, 2, 1): ag.on(g, slot)
+        if g + 1 < NG: ag.start_z(g + 1); ag.start_x(g + 1)
+        for slot in (3, 7, 4, 8, 6, 10, 5, 9): ag.on(g, slot)
+        for slot in (11, 13, 12): ag.on(g, slot)
+    for g in range(NG):
+        for slot in range(14, 28): ag.on(g, slot)
+    ag.finish()
+
+def ag_call(wq, wk, wv, wo, wi, wu, space=pl.ANY):
+    bf = jnp.bfloat16
+    return pl.pallas_call(
+        ag_kernel,
+        out_shape=[jax.ShapeDtypeStruct((4, 768, 768), bf), jax.ShapeDtypeStruct((4, 768, 768), bf), jax.ShapeDtypeStruct((3072, 768), bf)],
+        in_specs=[pl.BlockSpec(memory_space=pl.ANY)] * 6,
+        out_specs=[pl.BlockSpec(memory_space=space)] * 3,
+        scratch_shapes=[pltpu.SemaphoreType.DMA((NG, 28)), pltpu.SemaphoreType.DMA((NG, 28)), pltpu.SemaphoreType.DMA((12,))],
+        compiler_params=pltpu.CompilerParams(collective_id=0, has_side_effects=True),
+    )(wq, wk, wv, wo, wi, wu)
+
+A, B, C, D = 0, 1, 2, 3
+SE, SD, SB, SC_, SZ, SFY, SFC = 0, 16, 20, 24, 28, 31, 32
+NS = 34
+
+class RS:
+    def __init__(self, grad, S, E, Dr, Br, Cr, Zr, acc, fin, send, recv):
+        self.grad = grad; self.S=S; self.E=E; self.Dr=Dr; self.Br=Br; self.Cr=Cr; self.Zr=Zr; self.acc=acc; self.fin=fin
+        self.send=send; self.recv=recv
+        self.z,self.x,self.y,self.c = coords()
+        self.pending=[]
+    def dev(self, z,x,y,c): return (z*2+x, y*2+c)
+    def zp(self, dz): return lax.rem(self.z+dz,4)
+    def xfirst(self, g, dz): return dz in ((0,1,3) if g % 2 == 0 else (0, 2))
+    def piece(self, role, dz, c):
+        x = self.x if role in (A, C) else 1 - self.x
+        y = self.y if role in (A, B) else 1 - self.y
+        return self.zp(dz)*2 + x, y*2 + c
+    def copy(self, src, dst, g, slot, dev):
+        cp = pltpu.make_async_remote_copy(src_ref=src, dst_ref=dst, send_sem=self.send.at[g, slot], recv_sem=self.recv.at[g, slot], device_id=dev, device_id_type=MESH)
+        cp.start(); self.pending.append(cp)
+    def wait(self, g, slot, ref):
+        pltpu.make_async_remote_copy(src_ref=ref, dst_ref=ref, send_sem=self.send.at[g, slot], recv_sem=self.recv.at[g, slot], device_id=self.dev(self.z,self.x,self.y,1-self.c), device_id_type=MESH).wait_recv()
+    def nx(self): return self.dev(self.z,1-self.x,self.y,self.c)
+    def ny(self): return self.dev(self.z,self.x,1-self.y,self.c)
+    def nc(self): return self.dev(self.z,self.x,self.y,1-self.c)
+    def start(self, g):
+        for role in (D, B, C, A):
+            for dz in (1,2,3,0):
+                d,q = self.piece(role, dz, 1-self.c)
+                self.copy(self.grad(g,d,q), self.E.at[g, role*4+dz], g, SE+role*4+dz, self.nc())
+    def add(self, dst, refs, f32=False):
+        def step(i, _):
+            r = pl.ds(pl.multiple_of(i*32,32),32)
+            t = refs[0][r,:].astype(jnp.float32)
+            for a in refs[1:]: t = t + a[r,:].astype(jnp.float32)
+            dst[r,:] = t.astype(dst.dtype)
+            return 0
+        lax.fori_loop(0,3,step,0)
+    def mine(self, g, role, dz):
+        d,q = self.piece(role, dz, self.c)
+        i = role*4+dz
+        self.wait(g, SE+i, self.E.at[g,i])
+        return [self.grad(g,d,q), self.E.at[g,i]]
+    def diag(self, g, dz):
+        i = D*4+dz
+        self.add(self.S.at[g,i], self.mine(g,D,dz))
+        self.copy(self.S.at[g,i], self.Dr.at[g,dz], g, SD+dz, self.nx() if self.xfirst(g,dz) else self.ny())
+    def bsend(self, g, dz):
+        i = B*4+dz
+        refs = self.mine(g,B,dz)
+        if not self.xfirst(g,dz):
+            self.wait(g, SD+dz, self.Dr.at[g,dz]); refs.append(self.Dr.at[g,dz])
+        self.add(self.S.at[g,i], refs)
+        self.copy(self.S.at[g,i], self.Br.at[g,dz], g, SB+dz, self.nx())
+    def csend(self, g, dz):
+        i = C*4+dz
+        refs = self.mine(g,C,dz)
+        if self.xfirst(g,dz):
+            self.wait(g, SD+dz, self.Dr.at[g,dz]); refs.append(self.Dr.at[g,dz])
+        self.add(self.S.at[g,i], refs)
+        self.copy(self.S.at[g,i], self.Cr.at[g,dz], g, SC_+dz, self.ny())
+    def asend(self, g, dz):
+        i = A*4+dz
+        refs = self.mine(g,A,dz)
+        self.wait(g, SB+dz, self.Br.at[g,dz]); self.wait(g, SC_+dz, self.Cr.at[g,dz])
+        refs += [self.Br.at[g,dz], self.Cr.at[g,dz]]
+        if dz == 0:
+            self.add(self.acc.at[g], refs)
+        else:
+            self.add(self.S.at[g,i], refs)
+            self.copy(self.S.at[g,i], self.Zr.at[g,3-dz], g, SZ+3-dz, self.dev(self.zp(dz),self.x,self.y,self.c))
+    def total(self, g):
+        refs=[self.acc.at[g]]
+        for k in range(3):
+            self.wait(g, SZ+k, self.Zr.at[g,k]); refs.append(self.Zr.at[g,k])
+        q = self.y*2+self.c
+        f = self.fin.at[g,q]
+        self.add(f, refs)
+        self.copy(f, f, g, SFY, self.ny())
+        self.copy(f, f, g, SFC, self.nc())
+    def fwd(self, g):
+        f = self.fin.at[g,(1-self.y)*2+self.c]
+        self.wait(g, SFY, f)
+        self.copy(f, f, g, SFC+1, self.nc())
+    def last(self, g):
+        self.wait(g, SFC, self.fin.at[g, self.y*2+1-self.c])
+        self.wait(g, SFC+1, self.fin.at[g, (1-self.y)*2+1-self.c])
+    def finish(self):
+        for cp in self.pending: cp.wait_send()
+
+def rs_kernel(g0, g1, g2, oq, ok, ov, oo, oi, ou, S, E, Dr, Br, Cr, Zr, acc, fin, send, recv):
+    def grad(g,d,q):
+        if g == 0: return g0.at[q, pl.ds(pl.multiple_of(d*96,96),96), :]
+        if g == 1: return g1.at[q, pl.ds(pl.multiple_of(d*96,96),96), :]
+        return g2.at[pl.ds(pl.multiple_of(d*384+q*96,96),96), :]
+    rs = RS(grad,S,E,Dr,Br,Cr,Zr,acc,fin,send,recv)
+    barrier([rs.nx(), rs.ny(), rs.nc()] + [rs.dev(rs.zp(k),rs.x,rs.y,rs.c) for k in (1,2,3)])
+    order = (2, 1, 0)
+    for g in order: rs.start(g)
+    for g in order:
+        for dz in (1,2,3,0): rs.diag(g,dz)
+        for dz in (1,2,3,0):
+            if rs.xfirst(g,dz): rs.bsend(g,dz)
+            else: rs.csend(g,dz)
+        for dz in (1,2,3,0):
+            if rs.xfirst(g,dz): rs.csend(g,dz)
+            else: rs.bsend(g,dz)
+        if g != 2:
+            for dz in (1,2,3,0): rs.asend(g+1,dz)
+    for dz in (1,2,3,0): rs.asend(0,dz)
+    for g in order: rs.total(g)
+    for g in order: rs.fwd(g)
+    for g in order: rs.last(g)
+    def out(o, g, q, lanes=None, rows=None):
+        def step(i,_):
+            r = pl.ds(pl.multiple_of(i*32,32),32)
+            v = fin[g,q,r,:].astype(jnp.float32)
+            if lanes is not None: o[r, lanes:lanes+768] = v
+            else: o[pl.ds(pl.multiple_of(rows+i*32,32),32),:] = v
+            return 0
+        lax.fori_loop(0,3,step,0)
+    for q,o in enumerate((oq,ok,ov,oo)): out(o,0,q,rows=0)
+    for q in range(4): out(oi,1,q,lanes=q*768)
+    for q in range(4): out(ou,2,q,rows=q*96)
+    rs.finish()
+
+def rs_call(g0,g1,g2):
+    bf=jnp.bfloat16; f=jnp.float32
+    V=pltpu.VMEM
+    return pl.pallas_call(
+        rs_kernel,
+        out_shape=[jax.ShapeDtypeStruct((96,768),f)]*4+[jax.ShapeDtypeStruct((96,3072),f), jax.ShapeDtypeStruct((384,768),f)],
+        in_specs=[pl.BlockSpec(memory_space=pltpu.VMEM)]*3,
+        out_specs=[pl.BlockSpec(memory_space=pltpu.VMEM)]*6,
+        scratch_shapes=[V((NG,16,96,768),bf),V((NG,16,96,768),bf),V((NG,4,96,768),bf),V((NG,4,96,768),bf),V((NG,4,96,768),bf),V((NG,3,96,768),bf),V((NG,96,768),f),V((NG,4,96,768),bf),
+            pltpu.SemaphoreType.DMA((NG,NS)), pltpu.SemaphoreType.DMA((NG,NS))],
+        compiler_params=pltpu.CompilerParams(collective_id=1, has_side_effects=True, vmem_limit_bytes=60<<20),
+    )(g0,g1,g2)
+
+def fast_body(tokens, segment_ids, key_mask, w_query, b_query, w_key, w_value, b_value, w_attn_out, b_attn_out, gain_attn,
+              shift_attn, w_inner, b_inner, w_outer, b_outer, gain_ffn, shift_ffn, grad_output):
+    f32, bf16 = jnp.float32, jnp.bfloat16
+    seq_count, local_len, width = tokens.shape
+    head_count = H // lax.axis_size("sp")
+    score_scale = HD ** (-0.5)
+    a0, a1, a2 = ag_call(w_query, w_key, w_value, w_attn_out, w_inner, w_outer)
+    wq, wk, wv, wo = a0[0], a0[1], a0[2], a0[3]
+    small = jnp.concatenate([jnp.stack([b_query, b_value, b_attn_out, gain_attn, shift_attn, b_outer, gain_ffn, shift_ffn]),
+                             b_inner.reshape(4, 96)])
+    smalls = lax.all_gather(small, "dp", axis=0)
+    vec = lambda i: smalls[:, i].reshape(-1)
+    bq, bv, bo, ga, sa, bu, gf, sf = [vec(i) for i in range(8)]
+    bi = smalls[:, 8:12].reshape(-1)
+    rows = tokens.reshape(-1, width)
+    shape3 = (seq_count, local_len, width)
+    a2h = lambda t: lax.all_to_all(t.reshape(shape3), "sp", split_axis=2, concat_axis=1, tiled=True)
+    a2t = lambda t: lax.all_to_all(t, "sp", split_axis=1, concat_axis=2, tiled=True).reshape(-1, width)
+    query = a2h((matmul(rows, wq) + bq).astype(bf16))
+    keys = a2h(matmul(rows, wk).astype(bf16))
+    values = a2h((matmul(rows, wv) + bv).astype(bf16))
+    attended, log_total = lax.map(lambda m: attend_forward(*m, head_count, score_scale), (query, keys, values, segment_ids, key_mask))
+    merged = a2t(attended)
+    first_sum = rows + (matmul(merged, wo) + bo)
+    hidden, pull1 = jax.vjp(normalize, first_sum, ga.astype(f32), sa.astype(f32))
+    hidden_low = hidden.astype(bf16)
+    inner = jnp.concatenate([matmul(hidden_low, a1[i]) for i in range(4)], axis=1) + bi
+    active, gpull = jax.vjp(gelu_exact, inner)
+    active_low = active.astype(bf16)
+    second = hidden + (matmul(active_low, a2) + bu)
+    result, pull2 = jax.vjp(normalize, second, gf.astype(f32), sf.astype(f32))
+    layer_out = result.astype(bf16).reshape(shape3)
+    grad_second, g_gf, g_sf = pull2(grad_output.reshape(-1, width).astype(f32))
+    gol = grad_second.astype(bf16)
+    g_bu = column_sum(gol)
+    g_wu = left_trans(active_low, gol).astype(bf16)
+    (grad_inner,) = gpull(right_trans(gol, a2))
+    gil = grad_inner.astype(bf16)
+    g_bi = column_sum(gil)
+    g_wi = jnp.stack([left_trans(hidden_low, gil[:, i * 768:(i + 1) * 768]).astype(bf16) for i in range(4)])
+    back = sum(right_trans(gil[:, i * 768:(i + 1) * 768], a1[i]) for i in range(4))
+    grad_first, g_ga, g_sa = pull1(grad_second + back)
+    gbl = grad_first.astype(bf16)
+    g_bo = column_sum(gbl)
+    g_wo = left_trans(merged, gbl).astype(bf16)
+    gheads = a2h(right_trans(gbl, wo).astype(bf16))
+    hq, hk, hv = lax.map(lambda m: attend_backward(*m, head_count, score_scale),
+                         (query, keys, values, gheads, log_total, segment_ids, key_mask))
+    gq, gk, gv = a2t(hq), a2t(hk), a2t(hv)
+    g_w0 = jnp.stack([left_trans(rows, gq).astype(bf16), left_trans(rows, gk).astype(bf16), left_trans(rows, gv).astype(bf16), g_wo])
+    g_bq, g_bv = column_sum(gq), column_sum(gv)
+    grad_tokens = (grad_first + right_trans(gq, wq) + right_trans(gk, wk) + right_trans(gv, wv)).astype(bf16).reshape(shape3)
+    oq, ok, ov, oo, oi, ou = rs_call(g_w0, g_wi, g_wu)
+    vecs = jnp.stack([g_bq, g_bv, g_bo, g_ga, g_sa, g_bu, g_gf, g_sf])
+    vecs = jnp.concatenate([vecs, g_bi.reshape(4, 768)])
+    vecs = lax.psum(vecs, ("dp", "sp"))
+    d = lax.axis_index("dp")
+    cut = lax.dynamic_slice(vecs[:8], (0, d * 96), (8, 96))
+    s_bi = lax.dynamic_slice(vecs[8:].reshape(-1), (d * 384,), (384,))
+    return (layer_out, grad_tokens, oq, cut[0], ok, ov, cut[1], oo, cut[2], cut[3], cut[4], oi, s_bi, ou, cut[5], cut[6], cut[7])
+
+
 def solution(mesh):
     return jax.shard_map(
-        body,
+        fast_body if mesh.shape['dp'] == 8 and mesh.shape['sp'] == 4 else body,
         mesh=mesh,
         in_specs=(
             P("dp", "sp", None),

time: 1630 us -> 678 us (0.42)
  waiting for transfers between devices: 952 us -> 53.8 us
  Pallas kernels: 0 us -> 219 us
  blocking collectives: 171 us -> 73.1 us
  other arithmetic: 138 us -> 54.3 us
  local copies, waits for them, and re-layouts: 126 us -> 88.2 us
  starting transfers between devices: 60 us -> 29.9 us
    reduce_scatter x6 -> x0, waiting for transfers between devices: 605 us -> none  [the longest x1 163 us: body(): lax.psum_scatter(g_wi, 'dp', scatter_dimension=0, tiled=True)]
    all_gather x12 -> x0, waiting for transfers between devices: 322 us -> none  [the longest x2 136 us: layer_pass(): lax.all_gather(w_outer, 'dp', axis=0, tiled=True)]
    pallas_call x0 -> x2, Pallas kernels: none -> 219 us  [the longest x1 123 us: ag_call(): pl.pallas_call(ag_kernel, out_shape=[jax.ShapeDtypeStruct((4, 768, 768),...]
    while x2 -> x0, blocking collectives: 75.3 us -> none
    while x24 -> x4, other arithmetic: 63.1 us -> 0.01 us
    while x400 -> x166, local copies, waits for them, and re-layouts: 78.2 us -> 17.5 us  [the longest x3 7.37 us: fast_body(): lax.map(lambda m: attend_backward(*m, head_count, score_scale), (query, k...]
    all_to_all x16 -> x8, waiting for transfers between devices: 13.8 us -> 53.8 us  [the longest x4 34.3 us: fast_body(): lax.all_to_all(t.reshape(shape3), 'sp', split_axis=2, concat_axis=1, tile...]
    unnamed x1 -> x0, blocking collectives: 35.7 us -> none
  transfers between devices with their start and end apart: 35 -> 8, of which waited for: 18 -> 7; matrix products, arithmetic and copies ran while one was open for 16% -> 8% of each run, Pallas kernels for 0% -> 0%
where the time goes in v1:
time: 678 us; the launch traced here: 666 us
  Pallas kernels  219 us (32%)
  matrix products  145 us (21%)
  local copies, waits for them, and re-layouts  88.2 us (13%)
  blocking collectives  73.1 us (11%)
  other arithmetic  54.3 us (8%)
  waiting for transfers between devices  53.8 us (8%)
  starting transfers between devices  29.9 us (4%)
    pallas_call x1, Pallas kernels, ag_call(): pl.pallas_call(ag_kernel, out_shape=[jax.ShapeDtypeStruct((4, 768, 768),...  123 us
    pallas_call x1, Pallas kernels, rs_call(): pl.pallas_call(rs_kernel, out_shape=[jax.ShapeDtypeStruct((96, 768), f)]...  96.2 us
    dot_general x9, matrix products, right_trans(): lax.dot_general(left, right, (((1,), (1,)), ((), ())), preferred_element_...  44.9 us
    psum x1, blocking collectives, fast_body(): vecs = lax.psum(vecs, ('dp', 'sp'))  40.7 us
    all_to_all x4, waiting for transfers between devices, fast_body(): lax.all_to_all(t.reshape(shape3), 'sp', split_axis=2, concat_axis=1, tile...  34.3 us
    all_gather x1, blocking collectives, fast_body(): smalls = lax.all_gather(small, 'dp', axis=0)  32.4 us
    dot_general x9, matrix products, left_trans(): lax.dot_general(left, right, (((0,), (0,)), ((), ())), preferred_element_...  24.5 us
    all_to_all x4, waiting for transfers between devices, fast_body(): lax.all_to_all(t, 'sp', split_axis=1, concat_axis=2, tiled=True)  19.5 us
  transfers between devices with their start and end apart: 8, of which 7 were waited for; matrix products, arithmetic and copies ran while one was open for 8% of the time, Pallas kernels for 0%

profile of v1, /device:TPU:0, one launch (start us, length us, event | category | flops | bytes accessed | tf_op | source)
XLA Modules:
  0.0 666.4 jit_solution(7575579904075577514)
XLA Ops:
  2.2 32.4 %all-gather.1 = bf16[8,12,96]{2,1,0:T(8,128)(2,1)S(1)} all-gather(bf16[1,12,96]{2,1,0:T(8,128)(2,1)S(1)} %bitcast.395), channel_id=2, replica_groups=mesh['dp'=8,'sp'=4] {'dp'}, dimensions={0}, use_global_device_ids=true | all-gather | bytes 20736 | tf_op jit(solution)/shard_map/all_gather | solution.py:693
  36.0 122.8 %shard_map.314 = (bf16[4,768,768]{2,1,0:T(8,128)(2,1)}, bf16[4,768,768]{2,1,0:T(8,128)(2,1)}, bf16[3072,768]{1,0:T(8,128)(2,1)}) custom-call(bf16[96,768]{1,0:T(8,128)(2,1)} %wq.1, bf16[96,768]{1,0:T(8,128)(2,1)} %wk.1, bf16[96,768]{1,0:T(8,128)(2,1)} %wv.1, bf16[96,768]{1,0:T(8,128)(2,1)} %wo.1, bf16[96,3072]{1,0:T(8,128)(2,1)} %wi.1, bf16[384,768]{1,0:T(8,128)(2,1)} %wu.1), custom_call_target="tpu_custom_call" | custom-call | tf_op jit(solution)/shard_map/pallas_call | solution.py:535
  170.4 7.7 %all-to-all-done = bf16[2,256,768]{1,0,2:T(2,128)(2,1)S(1)} async-done(((bf16[2,256,768]{1,0,2:T(2,128)(2,1)}), bf16[2,256,768]{1,0,2:T(2,128)(2,1)S(1)}, u32[]{:S(2)}, u32[]{:S(2)}) %all-to-all-start) | async-done | bytes 786464 | tf_op jit(solution)/shard_map/all_to_all | solution.py:699
  178.0 3.5 all-to-all-start.2
  185.4 7.7 %all-to-all-done.2 = bf16[2,256,768]{1,0,2:T(2,128)(2,1)S(1)} async-done(((bf16[2,256,768]{1,0,2:T(2,128)(2,1)}), bf16[2,256,768]{1,0,2:T(2,128)(2,1)S(1)}, u32[]{:S(2)}, u32[]{:S(2)}) %all-to-all-start.2) | async-done | bytes 786464 | tf_op jit(solution)/shard_map/all_to_all | solution.py:699
  197.1 11.2 %all-to-all-done.1 = bf16[2,256,768]{1,0,2:T(2,128)(2,1)S(1)} async-done(((bf16[2,256,768]{1,0,2:T(2,128)(2,1)}), bf16[2,256,768]{1,0,2:T(2,128)(2,1)S(1)}, u32[]{:S(2)}, u32[]{:S(2)}) %all-to-all-start.1) | async-done | bytes 786464 | tf_op jit(solution)/shard_map/all_to_all | solution.py:699
  209.5 39.0 %while.54 = (s32[]{:T(128)}, bf16[2,1024,192]{2,1,0:T(8,128)(2,1)}, f32[2,2,3,512]{3,2,1,0:T(4,128)}, bf16[2,1024,192]{1,2,0:T(8,128)(2,1)S(1)}, s32[2,1024]{1,0...) while((s32[]{:T(128)}, bf16[2,1024,192]{2,1,0:T(8,128)(2,1)}, ...), condition=%wide.region_5.6_spmd, body=%wide.region_0.5_spmd.sunk | while | flops 423724544 | bytes 30094772 | solution.py:704
  212.6 13.7 %while.57 = (s32[]{:T(128)}, bf16[2,512,192]{1,2,0:T(8,128)(2,1)}, f32[2,3,512]{2,1,0:T(4,128)S(1)}, s32[2,512]{1,0:T(2,128)S(1)}, s32[1024]{0:T(1024)S(1)}, /*i...) while((s32[]{:T(128)}, bf16[2,512,192]{1,2,0:T(8,128)(2,1)}, ...), condition=%wide.region_4.4_spmd, body=%wide.region_1.3_spmd.sunk | while | flops 423722496 | bytes 24195732 | solution.py:87
  232.1 13.7 %while.57 = (s32[]{:T(128)}, bf16[2,512,192]{1,2,0:T(8,128)(2,1)}, f32[2,3,512]{2,1,0:T(4,128)S(1)}, s32[2,512]{1,0:T(2,128)S(1)}, s32[1024]{0:T(1024)S(1)}, /*i...) while((s32[]{:T(128)}, bf16[2,512,192]{1,2,0:T(8,128)(2,1)}, ...), condition=%wide.region_4.4_spmd, body=%wide.region_1.3_spmd.sunk | while | flops 423722496 | bytes 24195732 | solution.py:87
  251.8 3.8 all-to-all-start.3
  256.8 13.1 %all-to-all-done.3 = bf16[2,1024,192]{2,0,1:T(2,128)(2,1)S(1)} async-done(((bf16[2,1024,192]{2,0,1:T(2,128)(2,1)}), bf16[2,1024,192]{2,0,1:T(2,128)(2,1)S(1)}, u32[]{:S(2)}, u32[]{:S(2)}) %all-to-all-start.3) | async-done | bytes 786464 | tf_op jit(solution)/shard_map/all_to_all | solution.py:700
  281.2 14.6 %multiply_convert_fusion.1 = (bf16[512,3072]{1,0:T(8,128)(2,1)S(1)}, f32[512,3072]{1,0:T(8,128)}) fusion(f32[3072]{0:T(1024)S(1)} %reshape.512, f32[512,768]{1,0:T(8,128)S(1)} %fusion.61, f32[512,768]{1,0:T(8,128)S(1)} %fusion.65, f32[512,768]{1,0:T(8,128)S(1)} %fusion.69, f32[512,768]{1,0:T(8,128)S(1)} %fusion.73), kind=kLoop, calls=%fused_computation.80 | loop fusion | flops 108527616 | bytes 15740928 | tf_op jit(solution)/shard_map/convert_element_type | solution.py:711
  302.6 21.0 %convert_reduce_fusion = (f32[3072]{0:T(1024)}, bf16[512,3072]{1,0:T(8,128)(2,1)}) fusion(f32[512,3072]{1,0:T(8,128)} %get-tuple-element.531, f32[3072]{0:T(1024)S(1)} %reshape.512, f32[512,768]{1,0:T(8,128)} %copy-done.25, f32[512,768]{1,0:T(8,128)S(1)} %copy-done.24, f32[512,768]{1,0:T(8,128)S(1)} %fusion.69, f32[512,768]{1,0:T(8,128)S(1)} %fusion.73, ...), kind=kOutput, calls=%fused_computation.78 | convolution fusion | flops 2447373312 | bytes 21258240 | tf_op jit(solution)/shard_map/dot_general | solution.py:41
  342.9 4.2 all-to-all-start.4
  351.1 7.7 %all-to-all-done.4 = bf16[2,256,768]{1,0,2:T(2,128)(2,1)} async-done(((bf16[2,256,768]{1,0,2:T(2,128)(2,1)}), bf16[2,256,768]{1,0,2:T(2,128)(2,1)}, u32[]{:S(2)}, u32[]{:S(2)}) %all-to-all-start.4) | async-done | bytes 786464 | tf_op jit(solution)/shard_map/all_to_all | solution.py:699
  362.1 85.2 %while.56 = (s32[]{:T(128)}, bf16[2,1024,192]{2,1,0:T(8,128)(2,1)}, bf16[2,1024,192]{1,2,0:T(8,128)(2,1)}, bf16[2,1024,192]{1,2,0:T(8,128)(2,1)}, bf16[2,1024,19...) while((s32[]{:T(128)}, bf16[2,1024,192]{2,1,0:T(8,128)(2,1)}, ...), condition=%wide.region_18.19_spmd, body=%wide.region_14.18_spmd.sunk | while | flops 1033897472 | bytes 150009424 | solution.py:729
  367.9 31.2 %while.58 = (s32[]{:T(128)}, f32[1024,3,64]{0,2,1:T(8,128)}, f32[1024,3,64]{0,2,1:T(8,128)}, bf16[2,512,192]{1,2,0:T(8,128)(2,1)}, bf16[2,512,3,64]{1,3,2,0:T(8,...) while((s32[]{:T(128)}, f32[1024,3,64]{0,2,1:T(8,128)}, ...), condition=%wide.region_17.17_spmd.clone, body=%wide.region_15.16_spmd.clone.sunk | while | flops 1033502208 | bytes 119148632 | solution.py:134
  379.3 3.9 fusion.199
  394.9 4.2 fusion.199
  410.5 31.2 %while.58 = (s32[]{:T(128)}, f32[1024,3,64]{0,2,1:T(8,128)}, f32[1024,3,64]{0,2,1:T(8,128)}, bf16[2,512,192]{1,2,0:T(8,128)(2,1)}, bf16[2,512,3,64]{1,3,2,0:T(8,...) while((s32[]{:T(128)}, f32[1024,3,64]{0,2,1:T(8,128)}, ...), condition=%wide.region_17.17_spmd.clone, body=%wide.region_15.16_spmd.clone.sunk | while | flops 1033502208 | bytes 119148632 | solution.py:134
  421.9 3.9 fusion.199
  437.5 4.2 fusion.199
  450.6 3.7 all-to-all-start.5
  463.3 5.4 all-to-all-done.5
  468.7 4.2 all-to-all-start.7
  476.1 6.8 %convolution_convert_fusion.g2 = bf16[3072,768]{1,0:T(8,128)(2,1)} fusion(bf16[512,3072]{1,0:T(8,128)(2,1)} %copy-done.22, bf16[512,768]{1,0:T(8,128)(2,1)S(1)} %copy-done.43), kind=kOutput, calls=%fused_computation.94 | convolution fusion | flops 2418278400 | bytes 8650752 | tf_op jit(solution)/shard_map/dot_general | solution.py:35
  487.5 3.5 all-to-all-start.6
  491.0 4.7 copy.113
  499.4 40.7 %psum.7 = f32[12,768]{1,0:T(8,128)S(1)} all-reduce(f32[12,768]{1,0:T(8,128)S(1)} %concatenate.11), channel_id=1, replica_groups=mesh['dp'=8,'sp'=4] {'dp','sp'}, use_global_device_ids=true, to_apply=%region_28.29 | all-reduce | flops 9216 | bytes 73728 | tf_op jit(solution)/shard_map/psum | solution.py:738
  555.2 4.1 pad_maximum_fusion
  559.3 96.2 %shard_map.315 = (f32[96,768]{1,0:T(8,128)}, f32[96,768]{1,0:T(8,128)}, f32[96,768]{1,0:T(8,128)}, f32[96,768]{1,0:T(8,128)}, f32[96,3072]{1,0:T(8,128)}, /*index=5*/f32[384,768]{1,0:T(8,128)}) custom-call(bf16[4,768,768]{2,1,0:T(8,128)(2,1)} %get-tuple-element.559.g0, bf16[4,768,768]{2,1,0:T(8,128)(2,1)} %get-tuple-element.560.g1, ...), custom_call_target="tpu_custom_call" | custom-call | tf_op jit(solution)/shard_map/pallas_call | solution.py:673
  656.8 4.2 add_convert_fusion.1
  (514 shorter events, 223.6 us)
Async XLA Ops:
  162.9 15.1 %all-to-all-start = ((bf16[2,256,768]{1,0,2:T(2,128)(2,1)}), bf16[2,256,768]{1,0,2:T(2,128)(2,1)S(1)}, u32[]{:S(2)}, u32[]{:S(2)}) async-start(bf16[2,256,768]{1,0,2:T(2,128)(2,1)} %copy.92), calls=%async_computation | async-start | bytes 1572864 | tf_op jit(solution)/shard_map/all_to_all | solution.py:699
  178.0 15.1 %all-to-all-start.2 = ((bf16[2,256,768]{1,0,2:T(2,128)(2,1)}), bf16[2,256,768]{1,0,2:T(2,128)(2,1)S(1)}, u32[]{:S(2)}, u32[]{:S(2)}) async-start(bf16[2,256,768]{1,0,2:T(2,128)(2,1)} %copy.98), calls=%async_computation.2 | async-start | bytes 1572864 | tf_op jit(solution)/shard_map/all_to_all | solution.py:699
  193.1 15.1 %all-to-all-start.1 = ((bf16[2,256,768]{1,0,2:T(2,128)(2,1)}), bf16[2,256,768]{1,0,2:T(2,128)(2,1)S(1)}, u32[]{:S(2)}, u32[]{:S(2)}) async-start(bf16[2,256,768]{1,0,2:T(2,128)(2,1)} %copy.95), calls=%async_computation.1 | async-start | bytes 1572864 | tf_op jit(solution)/shard_map/all_to_all | solution.py:699
  212.6 15.8 %copy-start.49 = (f32[2,2,3,512]{3,2,1,0:T(4,128)S(1)}, f32[2,2,3,512]{3,2,1,0:T(4,128)}, u32[]{:S(2)}) copy-start(f32[2,2,3,512]{3,2,1,0:T(4,128)} %get-tuple-element.1000) | copy-start | bytes 73732 | tf_op jit(solution)/shard_map/while
  232.1 15.8 %copy-start.49 = (f32[2,2,3,512]{3,2,1,0:T(4,128)S(1)}, f32[2,2,3,512]{3,2,1,0:T(4,128)}, u32[]{:S(2)}) copy-start(f32[2,2,3,512]{3,2,1,0:T(4,128)} %get-tuple-element.1000) | copy-start | bytes 73732 | tf_op jit(solution)/shard_map/while
  248.5 8.1 %copy-start.64 = (f32[8,96]{1,0:T(8,128)S(1)}, f32[8,96]{1,0:T(8,128)}, u32[]{:S(2)}) copy-start(f32[8,96]{1,0:T(8,128)} %get-tuple-element.425) | copy-start | bytes 9220
  248.5 8.2 %copy-start.63 = (f32[8,96]{1,0:T(8,128)S(1)}, f32[8,96]{1,0:T(8,128)}, u32[]{:S(2)}) copy-start(f32[8,96]{1,0:T(8,128)} %get-tuple-element.424) | copy-start | bytes 9220
  248.5 8.3 %copy-start.62 = (f32[8,96]{1,0:T(8,128)S(1)}, f32[8,96]{1,0:T(8,128)}, u32[]{:S(2)}) copy-start(f32[8,96]{1,0:T(8,128)} %get-tuple-element.431) | copy-start | bytes 9220
  251.8 18.2 %all-to-all-start.3 = ((bf16[2,1024,192]{2,0,1:T(2,128)(2,1)}), bf16[2,1024,192]{2,0,1:T(2,128)(2,1)S(1)}, u32[]{:S(2)}, u32[]{:S(2)}) async-start(bf16[2,1024,192]{2,0,1:T(2,128)(2,1)} %copy.101), calls=%async_computation.3 | async-start | bytes 2097152 | tf_op jit(solution)/shard_map/all_to_all | solution.py:700
  280.3 15.4 %copy-start.23 = (f32[512,768]{1,0:T(8,128)}, f32[512,768]{1,0:T(8,128)S(1)}, u32[]{:S(2)}) copy-start(f32[512,768]{1,0:T(8,128)S(1)} %fusion.65) | copy-start | bytes 4718596
  280.4 15.4 %slice-start.4 = ((s8[4718592]{0:T(1024)(128)(4,1)}), s8[4194304]{0:T(1024)(128)(4,1)S(1)}, s32[]{:S(2)}) async-start(s8[4718592]{0:T(1024)(128)(4,1)} %bitcast.404), calls=%async_computation.12 | async-start | bytes 8388608
  281.2 14.6 %copy-start.25 = (f32[512,768]{1,0:T(8,128)}, f32[512,768]{1,0:T(8,128)S(1)}, u32[]{:S(2)}) copy-start(f32[512,768]{1,0:T(8,128)S(1)} %fusion.61) | copy-start | bytes 4718596
  281.2 14.6 %slice-start.5 = ((s8[4718592]{0:T(1024)(128)(4,1)}), s8[524288]{0:T(1024)(128)(4,1)S(1)}, s32[]{:S(2)}) async-start(s8[4718592]{0:T(1024)(128)(4,1)} %bitcast.404), calls=%async_computation.13 | async-start | bytes 1048576
  302.6 21.0 %copy-start.42 = (bf16[512,768]{1,0:T(8,128)(2,1)}, bf16[512,768]{1,0:T(8,128)(2,1)S(1)}, u32[]{:S(2)}) copy-start(bf16[512,768]{1,0:T(8,128)(2,1)S(1)} %get-tuple-element.523) | copy-start | bytes 2359300
  334.1 8.8 %copy-start.55 = (f32[512]{0:T(512)}, f32[512]{0:T(512)S(1)}, u32[]{:S(2)}) copy-start(f32[512]{0:T(512)S(1)} %negate_multiply_fusion.1) | copy-start | bytes 6148
  342.9 15.9 %all-to-all-start.4 = ((bf16[2,256,768]{1,0,2:T(2,128)(2,1)}), bf16[2,256,768]{1,0,2:T(2,128)(2,1)}, u32[]{:S(2)}, u32[]{:S(2)}) async-start(bf16[2,256,768]{1,0,2:T(2,128)(2,1)} %copy.103), calls=%async_computation.4 | async-start | bytes 1572864 | tf_op jit(solution)/shard_map/all_to_all | solution.py:699
  450.6 18.1 %all-to-all-start.5 = ((bf16[2,1024,192]{2,0,1:T(2,128)(2,1)}), bf16[2,1024,192]{2,0,1:T(2,128)(2,1)S(1)}, u32[]{:S(2)}, u32[]{:S(2)}) async-start(bf16[2,1024,192]{2,0,1:T(2,128)(2,1)} %copy.108), calls=%async_computation.5 | async-start | bytes 2097152 | tf_op jit(solution)/shard_map/all_to_all | solution.py:700
  459.4 13.6 %copy-start.39 = (bf16[96,8,2,256]{3,1,2,0:T(8,128)(2,1)S(1)}, bf16[96,8,2,256]{3,1,2,0:T(8,128)(2,1)}, u32[]{:S(2)}) copy-start(bf16[96,8,2,256]{3,1,2,0:T(8,128)(2,1)} %copy-done.38) | copy-start | bytes 2359300
  463.3 12.6 %copy-start.61 = (f32[768]{0:T(1024)S(1)}, f32[768]{0:T(1024)}, u32[]{:S(2)}) copy-start(f32[768]{0:T(1024)} %get-tuple-element.524) | copy-start | bytes 9220
  463.3 12.6 %copy-start.60 = (f32[768]{0:T(1024)S(1)}, f32[768]{0:T(1024)}, u32[]{:S(2)}) copy-start(f32[768]{0:T(1024)} %get-tuple-element.419) | copy-start | bytes 9220
  463.3 12.6 %copy-start.59 = (f32[768]{0:T(1024)S(1)}, f32[768]{0:T(1024)}, u32[]{:S(2)}) copy-start(f32[768]{0:T(1024)} %get-tuple-element.423) | copy-start | bytes 9220
  463.3 12.7 %copy-start.69 = (f32[3072]{0:T(1024)S(1)}, f32[3072]{0:T(1024)}, u32[]{:S(2)}) copy-start(f32[3072]{0:T(1024)} %get-tuple-element.520) | copy-start | bytes 36868
  463.3 12.7 %copy-start.58 = (f32[768]{0:T(1024)S(1)}, f32[768]{0:T(1024)}, u32[]{:S(2)}) copy-start(f32[768]{0:T(1024)} %get-tuple-element.522) | copy-start | bytes 9220
  463.3 12.7 %copy-start.57 = (f32[768]{0:T(1024)S(1)}, f32[768]{0:T(1024)}, u32[]{:S(2)}) copy-start(f32[768]{0:T(1024)} %get-tuple-element.421) | copy-start | bytes 9220
  463.3 12.7 %copy-start.43 = (bf16[512,768]{1,0:T(8,128)(2,1)S(1)}, bf16[512,768]{1,0:T(8,128)(2,1)}, u32[]{:S(2)}) copy-start(bf16[512,768]{1,0:T(8,128)(2,1)} %copy-done.42) | copy-start | bytes 2359300
  468.7 18.7 %all-to-all-start.7 = ((bf16[2,1024,192]{2,0,1:T(2,128)(2,1)}), bf16[2,1024,192]{2,0,1:T(2,128)(2,1)}, u32[]{:S(2)}, u32[]{:S(2)}) async-start(bf16[2,1024,192]{2,0,1:T(2,128)(2,1)} %copy.112), calls=%async_computation.7 | async-start | bytes 2097152 | tf_op jit(solution)/shard_map/all_to_all | solution.py:700
  486.5 12.9 %copy-start.68 = (f32[1,768]{1,0:T(1,128)S(1)}, f32[1,768]{1,0:T(1,128)}, u32[]{:S(2)}) copy-start(f32[1,768]{1,0:T(1,128)} %reshape.504) | copy-start | bytes 9220
  487.5 59.2 %all-to-all-start.6 = ((bf16[2,1024,192]{2,0,1:T(2,128)(2,1)}), bf16[2,1024,192]{2,0,1:T(2,128)(2,1)S(1)}, u32[]{:S(2)}, u32[]{:S(2)}) async-start(bf16[2,1024,192]{2,0,1:T(2,128)(2,1)} %copy.110), calls=%async_computation.6 | async-start | bytes 2097152 | tf_op jit(solution)/shard_map/all_to_all | solution.py:700
  559.3 96.2 %slice-start.2 = ((f32[12,768]{1,0:T(8,128)}), f32[8,768]{1,0:T(8,128)S(1)}, s32[]{:S(2)}) async-start(f32[12,768]{1,0:T(8,128)} %copy-done.54), calls=%async_computation.10 | async-start | bytes 49152 | tf_op jit(solution)/shard_map/slice | solution.py:740
  559.3 96.9 %slice-start.3 = ((f32[12,768]{1,0:T(8,128)}), f32[4,768]{1,0:T(4,128)S(1)}, s32[]{:S(2)}) async-start(f32[12,768]{1,0:T(8,128)} %copy-done.54), calls=%async_computation.11 | async-start | bytes 24576 | tf_op jit(solution)/shard_map/slice | solution.py:741
  559.3 97.5 %copy-start.17 = (f32[512,768]{1,0:T(8,128)S(1)}, f32[512,768]{1,0:T(8,128)}, u32[]{:S(2)}) copy-start(f32[512,768]{1,0:T(8,128)} %copy-done.16) | copy-start | bytes 4718596
  559.3 97.5 %copy-start.56 = (f32[512]{0:T(512)S(1)}, f32[512]{0:T(512)}, u32[]{:S(2)}) copy-start(f32[512]{0:T(512)} %copy-done.55) | copy-start | bytes 6148
  (107 other events, 387.7 us)
